TPU v7x, 256 devices: a whole 4x4x8 slice. The times are simulated.
256 devices in a mesh: dp: 64 (over x, z, core), mp: 4 (over y).
Axes of the slice: x: 4, y: 4, z: 8, core: 2. Of those that a mesh axis runs over, the one named last changes fastest.
Arguments:
- history: bfloat16 [1024, 32, 1024], P('dp', None, 'mp'), may hold values from -6 to 6
- lengths: int32 [1024], replicated, may hold values from 1 to 32, 16384 in all
- source: int32 [1024], replicated, may hold values from 0 to 1023, as said below
- owners: int32 [32768, 8], P(('dp', 'mp')), may hold values from 0 to 255, all different within a row; in each aligned block of 128 rows (0 to 127, 128 to 255, ...) at most 6 rows name the same one
- item_rows: int32 [32768, 8], P(('dp', 'mp')), may hold values from 0 to 511
- catalogue: bfloat16 [131072, 1024], P(('dp', 'mp')), may hold values from -6 to 6
- w_in: bfloat16 [4, 1024, 1024], P(None, None, 'mp'), may hold values from -0.1875 to 0.1875
- w_out: bfloat16 [1024, 1024], P('mp'), may hold values from -0.1875 to 0.1875
Outputs:
- w_in_grad: float32 [4, 1024, 1024], P(None, 'dp', 'mp')
- w_out_grad: float32 [1024, 1024], P('mp', 'dp')
- cat_grad: float32 [131072, 1024], P(('dp', 'mp'))
Inputs may be any that keep to these rules, and one draw needn't show every extreme that they name: `source`: a permutation; balanced slot k lies on index k // 16 of dp, and the 16 histories that start on one index of dp go to one index of dp at most (16 + 64 - 1) // 64 at a time, that many for some index. Each event names 8 different owners, column 0 the positive item's; the events of one device (aligned blocks of 128) name one owner at most 6 times.
All inputs are finite; a program needn't handle non-finite values.
Results may differ from a plain program's by a relative error of at most 0.017.
Values may be sent and summed in bfloat16 or wider, within the bound.
A program may use at most 128 MiB of HBM per device.

v0:
```python
import jax
import jax.numpy as jnp
from jax import lax
from jax.sharding import PartitionSpec as P

DH = 128
cosine_divisor = 0.05
epsilon_norm = 1e-05
epsilon_unit = 1e-06


def normalize(rows_in):
    centered = rows_in - jnp.mean(rows_in, axis=-1, keepdims=True)
    spread = jnp.mean(centered * centered, axis=-1, keepdims=True)
    return centered / jnp.sqrt(spread + epsilon_norm)


def attend(projected, length_here):
    gating = projected[0]
    values = projected[1]
    queries = projected[2]
    key_rows = projected[3]
    steps_n = projected.shape[1]
    scores = jnp.einsum(
        "thd,shd->hts", queries, key_rows, preferred_element_type=jnp.float32
    ) / jnp.sqrt(jnp.float32(projected.shape[3]))
    places = jnp.arange(steps_n, dtype=jnp.int32)
    allowed = (places[None, :] <= places[:, None]) & (places[None, :] < length_here)
    weights = jnp.where(
        allowed[None], jax.nn.silu(scores) / length_here.astype(jnp.float32), 0.0
    ).astype(jnp.bfloat16)
    mixed_out = jnp.einsum("hts,shd->thd", weights, values, preferred_element_type=jnp.float32)
    return (normalize(mixed_out) * gating.astype(jnp.float32)).astype(jnp.bfloat16)


def loss_block(out_rows, valid_rows, fetched):
    out_norm = jnp.sqrt(jnp.sum(out_rows * out_rows, axis=-1, keepdims=True) + epsilon_unit)
    request_unit_vector = out_rows / out_norm
    item_f = fetched.astype(jnp.float32)
    item_norm = jnp.sqrt(jnp.sum(item_f * item_f, axis=-1, keepdims=True) + epsilon_unit)
    catalog_unit_vector = item_f / item_norm
    cosine_match_raw = (
        jnp.einsum("qn,qgn->qg", request_unit_vector, catalog_unit_vector) / cosine_divisor
    )
    expo = jnp.exp(cosine_match_raw)
    probs = expo / jnp.sum(expo, axis=-1, keepdims=True)
    column = jnp.arange(cosine_match_raw.shape[1], dtype=jnp.int32)
    exponent_shares = (probs - (column[None, :] == 0).astype(jnp.float32)) * valid_rows[
        :, None
    ].astype(jnp.float32)
    request_unit_vector_slope = (
        jnp.einsum("as,asy->ay", exponent_shares, catalog_unit_vector) / cosine_divisor
    )
    out_grad = (
        request_unit_vector_slope
        - request_unit_vector
        * jnp.sum(request_unit_vector * request_unit_vector_slope, axis=-1, keepdims=True)
    ) / out_norm
    catalog_unit_vector_slope = (
        exponent_shares[:, :, None] * request_unit_vector[:, None, :] / cosine_divisor
    )
    item_grad = (
        catalog_unit_vector_slope
        - catalog_unit_vector
        * jnp.sum(catalog_unit_vector * catalog_unit_vector_slope, axis=-1, keepdims=True)
    ) / item_norm
    return (out_grad, item_grad)


def silu_slope(preact):
    sigma = jax.nn.sigmoid(preact)
    return sigma * (1.0 + preact * (1.0 - sigma))


def earlier_same(labels):
    order_ids = jnp.arange(labels.shape[0], dtype=jnp.int32)
    same = (labels[None, :] == labels[:, None]) & (order_ids[None, :] < order_ids[:, None])
    return jnp.sum(same.astype(jnp.int32), axis=1)


def per_device(history, lengths, source, owners, item_rows, catalogue, w_in, w_out):
    dp_count = lax.axis_size("dp")
    mp_count = lax.axis_size("mp")
    dev_count = dp_count * mp_count
    here_dp = lax.axis_index("dp")
    here_mp = lax.axis_index("mp")
    seq_dev, steps_n, cols_here = history.shape
    seq_total = source.shape[0]
    per_peer = (seq_dev + dp_count - 1) // dp_count
    target = (
        jnp.zeros((seq_total,), jnp.int32).at[source].set(jnp.arange(seq_total, dtype=jnp.int32))
    )
    slot_ids = jnp.arange(seq_dev, dtype=jnp.int32)
    my_seqs = here_dp * seq_dev + slot_ids
    dest_dev = target[my_seqs] // seq_dev
    send_rank = earlier_same(dest_dev)
    outgoing = (
        jnp.zeros((dp_count, per_peer, steps_n, cols_here), jnp.bfloat16)
        .at[dest_dev, send_rank]
        .set(history)
    )
    arrived = lax.all_to_all(outgoing, "dp", split_axis=0, concat_axis=0, tiled=True)
    taken = source[my_seqs]
    anchor = taken // seq_dev
    anchor_block = anchor[:, None] * seq_dev + slot_ids[None, :]
    goes_here = target[anchor_block] // seq_dev == here_dp
    earlier = slot_ids[None, :] < (taken % seq_dev)[:, None]
    recv_rank = jnp.sum((goes_here & earlier).astype(jnp.int32), axis=1)
    counts = lengths[taken]
    local_rows = jnp.take(
        arrived.reshape(dp_count * per_peer, steps_n, cols_here),
        anchor * per_peer + recv_rank,
        axis=0,
    )
    features = lax.all_gather(local_rows, "mp", axis=2, tiled=True)
    rows_all = seq_dev * steps_n
    width = features.shape[2]
    flat_rows = features.reshape(rows_all, width)
    normed = normalize(flat_rows.astype(jnp.float32)).astype(jnp.bfloat16)
    preact = jnp.einsum("rd,cdh->crh", normed, w_in, preferred_element_type=jnp.float32)
    projected = jax.nn.silu(preact).astype(jnp.bfloat16)
    cols_heads = w_in.shape[2]
    heads_here = cols_heads // DH
    grouped = projected.reshape(4, seq_dev, steps_n, heads_here, DH)

    def run_all(inputs):
        return jax.vmap(attend, in_axes=(1, 0))(inputs, counts)

    gated, back = jax.vjp(run_all, grouped)
    gated_flat = gated.reshape(rows_all, cols_heads)
    partial_out = jnp.dot(gated_flat, w_out, preferred_element_type=jnp.float32)
    quarter = rows_all // mp_count
    summed = lax.psum(partial_out, "mp")
    out_rows = lax.dynamic_slice_in_dim(summed, here_mp * quarter, quarter, 0)
    out_rows = out_rows + lax.dynamic_slice_in_dim(flat_rows, here_mp * quarter, quarter, 0).astype(
        jnp.float32
    )
    position = here_mp * quarter + jnp.arange(quarter, dtype=jnp.int32)
    valid_rows = position % steps_n < counts[position // steps_n]
    top_n = owners.shape[1]
    asks = quarter * top_n
    capacity = max(2, (3 * asks + 2 * dev_count - 1) // (2 * dev_count))
    owner_flat = owners.reshape(-1)
    row_flat = item_rows.reshape(-1)
    rank_in = earlier_same(owner_flat)
    address = owner_flat * capacity + rank_in
    slot_table = (
        jnp.full((dev_count * capacity,), asks, jnp.int32)
        .at[address]
        .set(jnp.arange(asks, dtype=jnp.int32))
    )
    is_used = slot_table < asks
    safe_index = jnp.minimum(slot_table, asks - 1)
    wanted = jnp.where(is_used, row_flat[safe_index], 0).reshape(dp_count, mp_count, capacity)
    incoming = lax.all_to_all(
        lax.all_to_all(wanted, "dp", split_axis=0, concat_axis=0, tiled=True),
        "mp",
        split_axis=1,
        concat_axis=1,
        tiled=True,
    )
    incoming_flat = incoming.reshape(-1)
    looked = jnp.take(catalogue, incoming_flat, axis=0).reshape(dp_count, mp_count, capacity, width)
    returned = lax.all_to_all(
        lax.all_to_all(looked, "dp", split_axis=0, concat_axis=0, tiled=True),
        "mp",
        split_axis=1,
        concat_axis=1,
        tiled=True,
    )
    fetched = jnp.take(returned.reshape(dev_count * capacity, width), address, axis=0).reshape(
        quarter, top_n, width
    )
    out_grad, item_grad = loss_block(out_rows, valid_rows, fetched)
    item_flat = item_grad.reshape(asks, width)
    sending = jnp.where(is_used[:, None], jnp.take(item_flat, safe_index, axis=0), 0.0)
    landed = lax.all_to_all(
        lax.all_to_all(
            sending.reshape(dp_count, mp_count, capacity, width).astype(jnp.bfloat16),
            "dp",
            split_axis=0,
            concat_axis=0,
            tiled=True,
        ),
        "mp",
        split_axis=1,
        concat_axis=1,
        tiled=True,
    ).astype(jnp.float32)
    cat_grad = (
        jnp.zeros((catalogue.shape[0], width), jnp.float32)
        .at[incoming_flat]
        .add(landed.reshape(-1, width))
    )
    out_cotangent = lax.all_gather(out_grad.astype(jnp.bfloat16), "mp", axis=0, tiled=True)
    w_out_part = jnp.einsum(
        "rh,rd->hd", gated_flat, out_cotangent, preferred_element_type=jnp.float32
    )
    gated_cotangent = jnp.einsum(
        "rd,hd->rh", out_cotangent, w_out, preferred_element_type=jnp.float32
    ).astype(jnp.bfloat16)
    (grouped_cotangent,) = back(gated_cotangent.reshape(seq_dev, steps_n, heads_here, DH))
    projected_cotangent = grouped_cotangent.reshape(4, rows_all, cols_heads)
    preact_cotangent = (projected_cotangent.astype(jnp.float32) * silu_slope(preact)).astype(
        jnp.bfloat16
    )
    w_in_part = jnp.einsum(
        "rd,crh->cdh", normed, preact_cotangent, preferred_element_type=jnp.float32
    )
    w_in_grad, w_out_grad = (
        lax.psum_scatter(w_in_part, "dp", scatter_dimension=1, tiled=True),
        lax.psum_scatter(w_out_part, "dp", scatter_dimension=1, tiled=True),
    )
    return (w_in_grad, w_out_grad, cat_grad)


def solution(mesh):
    placed = (
        P("dp", None, "mp"),
        P(),
        P(),
        P(("dp", "mp"), None),
        P(("dp", "mp"), None),
        P(("dp", "mp"), None),
        P(None, None, "mp"),
        P("mp", None),
    )
    return jax.shard_map(
        per_device,
        mesh=mesh,
        in_specs=placed,
        out_specs=(P(None, "dp", "mp"), P("mp", "dp"), P(("dp", "mp"), None)),
        check_vma=False,
    )
```

profile of v0, /device:TPU:8, one launch (start us, length us, event | category | flops | bytes accessed | tf_op | source)
XLA Modules:
  0.0 688.2 jit_solution(856039338225278554)
XLA Ops:
  7.2 0.9 copy.110
  10.0 4.3 scatter_custom_fusion.2
  15.3 5.9 gather_fusion.5
  21.8 0.8 reshape.655
  22.6 11.9 %all-to-all-start.1 = ((s32[64,4,6]{2,1,0:T(4,128)}), s32[64,4,6]{2,1,0:T(4,128)S(1)}, u32[]{:S(2)}, u32[]{:S(2)}) async-start(s32[64,4,6]{2,1,0:T(4,128)} %reshape.655), calls=%async_computation.1 | async-start | bytes 262144 | tf_op jit(solution)/shard_map/all_to_all | solution.py:156
  35.3 4.3 scatter_custom_fusion
  40.4 4.4 all-to-all-done.1
  45.6 4.9 all-to-all-start.2
  50.6 1.1 broadcast.800
  51.7 2.7 scatter_fusion
  54.4 6.4 all-to-all-start
  62.7 5.8 gather_fusion.6
  68.6 6.2 gather.53
  74.8 2.6 broadcast_select_fusion
  77.4 7.9 %copy.116 = bf16[64,4,6,1024]{3,1,2,0:T(4,128)(2,1)} copy(bf16[64,4,6,1024]{3,2,1,0:T(8,128)(2,1)S(1)} %broadcast_select_fusion) | data formatting | bytes 6291456 | tf_op jit(solution)/shard_map/jit(_take)/select_n | solution.py:163
  85.2 3.5 all-to-all-done
  88.8 7.2 %all-to-all-start.3 = ((bf16[64,4,6,1024]{3,1,2,0:T(4,128)(2,1)}), bf16[64,4,6,1024]{3,1,2,0:T(4,128)(2,1)}, u32[]{:S(2)}, u32[]{:S(2)}) async-start(bf16[64,4,6,1024]{3,1,2,0:T(4,128)(2,1)} %copy.116), calls=%async_computation.3 | async-start | bytes 6291456 | tf_op jit(solution)/shard_map/all_to_all | solution.py:165
  96.0 1.4 gather_fusion.2
  97.7 1.8 gather_fusion.4
  101.8 27.1 %all-gather.3.cloned.1.call-done = bf16[16,32,1024]{2,1,0:T(8,128)(2,1)} async-done(((bf16[16,32,256]{2,1,0:T(8,128)(2,1)}), bf16[16,32,1024]{2,1,0:T(8,128)(2,1)}) %all-gather.3.cloned.1.call-update) | async-done | bytes 1048592 | tf_op jit(solution)/shard_map/all_gather | solution.py:115
  128.8 1.5 convert_reduce_fusion.1
  130.4 1.6 fusion.12
  132.2 2.8 fusion.16
  135.6 1.1 select_convert_fusion
  138.9 1.8 fusion.54
  140.8 27.9 %all-to-all-done.3 = bf16[64,4,6,1024]{3,1,2,0:T(4,128)(2,1)} async-done(((bf16[64,4,6,1024]{3,1,2,0:T(4,128)(2,1)}), bf16[64,4,6,1024]{3,1,2,0:T(4,128)(2,1)}, u32[]{:S(2)}, u32[]{:S(2)}) %all-to-all-start.3) | async-done | bytes 3145760 | tf_op jit(solution)/shard_map/all_to_all | solution.py:165
  168.6 5.3 copy.117
  173.9 5.4 all-to-all-start.4
  182.5 0.9 broadcast_in_dim.175
  183.5 1.9 fusion.89
  185.5 10.0 %compare_convert_fusion = f32[128]{0:T(128)S(1)} fusion(s32[]{:T(128)} %bitcast.39, s32[]{:T(128)} %bitcast.40, s32[]{:T(128)} %bitcast.41, s32[]{:T(128)} %bitcast.42, s32[]{:T(128)} %bitcast.43, s32[]{:T(128)} %bitcast.45, s32[]{:T(128)} %bitcast.44, s32[]{:T(128)} %bitcast.22, s32[]{:T(128)} %bitcast.24, s32[]{:T(128)} %bitcast.26, s32[]{:T(128)} %bitcast.28, ...), kind=kLoop, calls=%fused_computation.196 | loop fusion | flops 8064 | bytes 580 | tf_op jit(solution)/shard_map/convert_element_type | solution.py:50
  196.8 34.2 %all-reduce.8.cloned.1.call-done = f32[512,1024]{1,0:T(8,128)} async-done(((f32[512,1024]{1,0:T(8,128)}), f32[512,1024]{1,0:T(8,128)}) %all-reduce.8.cloned.1.call-update) | async-done | bytes 2097168 | tf_op jit(solution)/shard_map/psum | solution.py:133
  231.1 1.3 multiply_reduce_fusion.2
  232.3 2.0 fusion.50
  234.4 3.7 copy.118
  238.1 4.9 reshape.657
  243.0 5.3 gather_fusion.7
  248.3 2.5 fusion.2
  250.9 2.8 fusion.10
  254.0 1.7 fusion.7
  255.7 1.1 fusion.9
  257.3 1.7 fusion.6
  259.0 5.8 gather_fusion.8
  264.8 6.2 gather.58
  271.1 4.7 fusion.1
  275.8 4.2 copy.133
  279.9 5.8 all-to-all-start.5
  286.0 0.9 divide_convert_fusion.1
  286.9 28.9 %all-gather.5.cloned.1.call-done = bf16[512,1024]{1,0:T(8,128)(2,1)} async-done(((bf16[128,1024]{1,0:T(8,128)(2,1)}), bf16[512,1024]{1,0:T(8,128)(2,1)}) %all-gather.5.cloned.1.call-update) | async-done | bytes 1048592 | tf_op jit(solution)/shard_map/all_gather | solution.py:195
  315.8 1.7 fusion.26
  321.2 1.9 copy.127
  323.2 2.8 reshape.662
  326.0 6.1 convolution_bitcast_fusion
  332.2 5.2 copy.129
  337.4 21.5 %all-to-all-done.5 = bf16[64,4,6,1024]{3,1,2,0:T(4,128)(2,1)} async-done(((bf16[64,4,6,1024]{3,1,2,0:T(4,128)(2,1)}), bf16[64,4,6,1024]{3,1,2,0:T(4,128)(2,1)}, u32[]{:S(2)}, u32[]{:S(2)}) %all-to-all-start.5) | async-done | bytes 3145760 | tf_op jit(solution)/shard_map/all_to_all | solution.py:178
  358.9 5.4 copy.134
  364.3 6.6 all-to-all-start.6
  370.9 2.8 fusion.52
  375.0 163.0 %all-reduce.10.cloned.1.call-done = f32[4,1024,256]{2,0,1:T(4,128)} async-done(((f32[4,1024,256]{2,0,1:T(4,128)}), f32[4,1024,256]{2,0,1:T(4,128)}) %all-reduce.10.cloned.1.call-update) | async-done | bytes 4194320
  538.0 0.8 constant_dynamic-slice_fusion
  539.4 5.1 copy.135
  544.6 8.4 %reshape.790 = f32[1536,1024]{1,0:T(8,128)} reshape(f32[64,4,6,1024]{3,2,1,0:T(8,128)} %copy.135) | data formatting | bytes 12582912 | tf_op jit(solution)/shard_map/reshape | solution.py:193
  553.0 16.1 %scatter_custom_fusion.3 = f32[512,1024]{1,0:T(8,128)} fusion(s32[1536]{0:T(1024)} %copy-done.39, f32[1536,1024]{1,0:T(8,128)} %reshape.790, f32[]{:T(128)} %constant.182.clone.1), kind=kCustom, calls=%fused_computation.68 | custom fusion | flops 1572864 | bytes 2097664 | tf_op jit(solution)/shard_map/scatter-add | solution.py:193
  569.1 112.4 %reduce-scatter.2.cloned.1.call-done = f32[256,16]{0,1:T(8,128)} async-done(((f32[256,1024]{0,1:T(8,128)}), f32[256,16]{0,1:T(8,128)}) %reduce-scatter.2.cloned.1.call-update) | async-done | bytes 16400 | tf_op jit(solution)/shard_map/reduce_scatter | solution.py:212
  (203 shorter events, 23.9 us)
Async XLA Ops:
  7.2 125.0 %copy-start = (bf16[4,1024,256]{2,1,0:T(8,128)(2,1)S(1)}, bf16[4,1024,256]{2,1,0:T(8,128)(2,1)}, u32[]{:S(2)}) copy-start(bf16[4,1024,256]{2,1,0:T(8,128)(2,1)} %param.14) | copy-start | bytes 6291460
  8.2 0.6 copy-start.40
  9.3 5.1 copy-start.38
  9.4 0.6 copy-start.41
  14.4 6.8 copy-start.29
  14.4 6.8 copy-start.30
  15.3 19.3 %copy-start.3 = (s32[1024]{0:T(1024)S(1)}, s32[1024]{0:T(1024)}, u32[]{:S(2)}) copy-start(s32[1024]{0:T(1024)} %param.10) | copy-start | bytes 12292
  22.6 22.2 %all-to-all-start.1 = ((s32[64,4,6]{2,1,0:T(4,128)}), s32[64,4,6]{2,1,0:T(4,128)S(1)}, u32[]{:S(2)}, u32[]{:S(2)}) async-start(s32[64,4,6]{2,1,0:T(4,128)} %reshape.655), calls=%async_computation.1 | async-start | bytes 262144 | tf_op jit(solution)/shard_map/all_to_all | solution.py:156
  45.6 8.8 %all-to-all-start.2 = ((s32[4,1,384]{2,1,0:T(1,128)}), s32[4,1,384]{2,1,0:T(1,128)S(1)}, u32[]{:S(2)}, u32[]{:S(2)}) async-start(s32[4,1,384]{2,1,0:T(1,128)} %reshape.856), calls=%async_computation.2 | async-start | bytes 12288 | tf_op jit(solution)/shard_map/all_to_all | solution.py:155
  50.6 12.2 %copy-start.2 = (bf16[512,1024]{1,0:T(8,128)(2,1)S(1)}, bf16[512,1024]{1,0:T(8,128)(2,1)}, u32[]{:S(2)}) copy-start(bf16[512,1024]{1,0:T(8,128)(2,1)} %param.13) | copy-start | bytes 3145732
  54.4 34.4 %all-to-all-start = ((bf16[64,1,32,256]{3,2,1,0:T(8,128)(2,1)}), bf16[64,1,32,256]{3,2,1,0:T(8,128)(2,1)}, u32[]{:S(2)}, u32[]{:S(2)}) async-start(bf16[64,1,32,256]{3,2,1,0:T(8,128)(2,1)} %bitcast.239), calls=%async_computation | async-start | bytes 2097152 | tf_op jit(solution)/shard_map/all_to_all | solution.py:102
  62.7 5.9 copy-start.39
  88.8 79.9 %all-to-all-start.3 = ((bf16[64,4,6,1024]{3,1,2,0:T(4,128)(2,1)}), bf16[64,4,6,1024]{3,1,2,0:T(4,128)(2,1)}, u32[]{:S(2)}, u32[]{:S(2)}) async-start(bf16[64,4,6,1024]{3,1,2,0:T(4,128)(2,1)} %copy.116), calls=%async_computation.3 | async-start | bytes 6291456 | tf_op jit(solution)/shard_map/all_to_all | solution.py:165
  95.9 32.9 %all-gather.3.cloned.1.call-start = ((), (), s32[]{:S(2)}) async-start(), calls=%async_computation.8 | async-start | bytes 1310720 | tf_op jit(solution)/shard_map/all_gather | solution.py:115
  96.0 4.6 copy-start.4
  100.3 130.8 %all-reduce.8.cloned.1.call-start = ((), (), s32[]{:S(2)}) async-start(), calls=%async_computation.9 | async-start | bytes 4194304 | tf_op jit(solution)/shard_map/psum | solution.py:133
  101.2 0.5 copy-start.24
  101.2 34.4 %copy-start.47 = (f32[16]{0:T(128)}, f32[16]{0:T(128)S(1)}, u32[]{:S(2)}) copy-start(f32[16]{0:T(128)S(1)} %convert_element_type.130) | copy-start | bytes 196
  101.8 33.9 %copy-start.34 = (pred[16,32,32]{2,1,0:T(8,128)(4,1)}, pred[16,32,32]{2,1,0:T(8,128)(4,1)S(1)}, u32[]{:S(2)}) copy-start(pred[16,32,32]{2,1,0:T(8,128)(4,1)S(1)} %broadcast_and_fusion) | copy-start | bytes 49156
  128.8 3.4 copy-start.12
  130.4 4.6 copy-start.42
  132.2 2.8 copy-start.44
  135.2 1.6 copy-start.20
  135.2 1.5 copy-start.16
  135.3 1.4 copy-start.18
  135.6 2.6 copy-start.10
  136.8 4.0 copy-start.22
  136.8 2.1 copy-start.14
  137.2 1.1 copy-start.7
  137.6 0.7 copy-start.27
  138.3 2.5 copy-start.25
  173.9 60.4 %all-to-all-start.4 = ((bf16[64,4,6,1024]{3,0,2,1:T(8,128)(2,1)}), bf16[64,4,6,1024]{3,0,2,1:T(8,128)(2,1)S(1)}, u32[]{:S(2)}, u32[]{:S(2)}) async-start(bf16[64,4,6,1024]{3,0,2,1:T(8,128)(2,1)} %copy.117), calls=%async_computation.4 | async-start | bytes 6291456 | tf_op jit(solution)/shard_map/all_to_all | solution.py:164
  248.3 2.6 copy-start.5
  248.3 2.6 copy-start.33
  250.9 2.8 copy-start.36
  250.9 3.1 copy-start.9
  254.0 1.7 copy-start.37
  255.7 1.6 copy-start.6
  257.3 1.7 copy-start.31
  279.9 79.0 %all-to-all-start.5 = ((bf16[64,4,6,1024]{3,1,2,0:T(4,128)(2,1)}), bf16[64,4,6,1024]{3,1,2,0:T(4,128)(2,1)}, u32[]{:S(2)}, u32[]{:S(2)}) async-start(bf16[64,4,6,1024]{3,1,2,0:T(4,128)(2,1)} %copy.133), calls=%async_computation.6 | async-start | bytes 6291456 | tf_op jit(solution)/shard_map/all_to_all | solution.py:178
  285.7 30.1 %copy-start.15 = (bf16[256,1024]{1,0:T(8,128)(2,1)S(1)}, bf16[256,1024]{1,0:T(8,128)(2,1)}, u32[]{:S(2)}) copy-start(bf16[256,1024]{1,0:T(8,128)(2,1)} %param.15) | copy-start | bytes 1572868
  285.7 30.1 %all-gather.5.cloned.1.call-start = ((), (), s32[]{:S(2)}) async-start(), calls=%async_computation.10 | async-start | bytes 1310720 | tf_op jit(solution)/shard_map/all_gather | solution.py:195
  286.0 31.9 %copy-start.8 = (f32[16,32,2,128]{3,1,2,0:T(8,128)S(1)}, f32[16,32,2,128]{3,1,2,0:T(8,128)}, u32[]{:S(2)}) copy-start(f32[16,32,2,128]{3,1,2,0:T(8,128)} %copy-done.7) | copy-start | bytes 1572868
  286.0 31.9 %copy-start.11 = (f32[16,32,2,128]{3,2,1,0:T(2,128)S(1)}, f32[16,32,2,128]{3,2,1,0:T(2,128)}, u32[]{:S(2)}) copy-start(f32[16,32,2,128]{3,2,1,0:T(2,128)} %copy-done.10) | copy-start | bytes 1572868
  286.0 31.9 %copy-start.32 = (f32[16,32,2]{1,2,0:T(2,128)S(1)}, f32[16,32,2]{1,2,0:T(2,128)}, u32[]{:S(2)}) copy-start(f32[16,32,2]{1,2,0:T(2,128)} %get-tuple-element.29) | copy-start | bytes 12292
  286.9 31.5 %copy-start.28 = (f32[16,32,2]{1,2,0:T(2,128)S(1)}, f32[16,32,2]{1,2,0:T(2,128)}, u32[]{:S(2)}) copy-start(f32[16,32,2]{1,2,0:T(2,128)} %copy-done.27) | copy-start | bytes 12292
  286.9 31.6 %copy-start.26 = (f32[16,32,2]{1,2,0:T(2,128)S(1)}, f32[16,32,2]{1,2,0:T(2,128)}, u32[]{:S(2)}) copy-start(f32[16,32,2]{1,2,0:T(2,128)} %copy-done.25) | copy-start | bytes 12292
  286.9 251.1 %all-reduce.10.cloned.1.call-start = ((), (), s32[]{:S(2)}) async-start(), calls=%async_computation.12 | async-start | bytes 8388608
  317.8 1.3 copy-start.21
  317.8 1.3 copy-start.35
  317.8 1.3 copy-start.48
  317.8 1.3 copy-start.49
  319.2 1.0 copy-start.19
  319.2 1.2 copy-start.17
  319.2 1.4 copy-start.23
  323.2 2.9 copy-start.13
  323.2 2.9 copy-start.43
  323.2 2.9 copy-start.45
  364.3 175.2 %all-to-all-start.6 = ((bf16[64,4,6,1024]{3,0,2,1:T(8,128)(2,1)}), bf16[64,4,6,1024]{3,0,2,1:T(8,128)(2,1)S(1)}, u32[]{:S(2)}, u32[]{:S(2)}) async-start(bf16[64,4,6,1024]{3,0,2,1:T(8,128)(2,1)} %copy.134), calls=%async_computation.7 | async-start | bytes 6291456 | tf_op jit(solution)/shard_map/all_to_all | solution.py:177
  370.9 2.8 copy-start.46
  370.9 310.6 %reduce-scatter.2.cloned.1.call-start = ((), (), s32[]{:S(2)}) async-start(), calls=%async_computation.11 | async-start | bytes 1064960 | tf_op jit(solution)/shard_map/reduce_scatter | solution.py:212
  544.6 136.9 %copy-start.1 = (bf16[4,1024,256]{2,1,0:T(8,128)(2,1)S(1)}, bf16[4,1024,256]{2,1,0:T(8,128)(2,1)}, u32[]{:S(2)}) copy-start(bf16[4,1024,256]{2,1,0:T(8,128)(2,1)} %param.14) | copy-start | bytes 6291460
Sparse Core Ops, SparseCore 0:
  100.4 28.3 all-gather.2
  140.9 90.1 all-reduce.7
  288.3 27.4 all-gather.4
  337.5 200.3 all-reduce.9
  542.4 139.0 reduce-scatter.1
where the time goes:
time: 695 us; the launch traced here: 688 us
  waiting for transfers between devices  423 us (61%)
  local copies, waits for them, and re-layouts  123 us (18%)
  other arithmetic  55.8 us (8%)
  starting transfers between devices  48.5 us (7%)
  matrix products  21.9 us (3%)
  between operations  15.7 us (2%)
    unnamed x6, waiting for transfers between devices  163 us
    reduce_scatter x1, waiting for transfers between devices, per_device(): lax.psum_scatter(w_out_part, 'dp', scatter_dimension=1, tiled=True)  112 us
    psum x1, waiting for transfers between devices, per_device(): summed = lax.psum(partial_out, 'mp')  34.2 us
    all_gather x1, waiting for transfers between devices, per_device(): lax.all_gather(out_grad.astype(jnp.bfloat16), 'mp', axis=0, tiled=True)  28.9 us
    all_to_all x1, waiting for transfers between devices, per_device(): lax.all_to_all(looked, 'dp', split_axis=0, concat_axis=0, tiled=True)  27.9 us
    all_gather x1, waiting for transfers between devices, per_device(): features = lax.all_gather(local_rows, 'mp', axis=2, tiled=True)  27.1 us
    all_to_all x1, waiting for transfers between devices, per_device(): lax.all_to_all(sending.reshape(dp_count, mp_count, capacity, width).astyp...  21.5 us
    scatter-add x1, other arithmetic, per_device(): cat_grad = jnp.zeros((catalogue.shape[0], width), jnp.float32).at[incomin...  16.1 us
  transfers between devices with their start and end apart: 12, of which 9 were waited for; matrix products, arithmetic and copies ran while one was open for 20% of the time, Pallas kernels for 0%

commit v1 on v0

--- a/solution.py
+++ b/solution.py
@@ -7,6 +7,12 @@
 cosine_divisor = 0.05
 epsilon_norm = 1e-05
 epsilon_unit = 1e-06
+
+
+def summed_here(x, axis):
+    pieces = lax.all_gather(x, axis, axis=0, tiled=False)
+    total = pieces.sum(axis=0)
+    return total
 
 
 def normalize(rows_in):
@@ -130,7 +136,7 @@
     gated_flat = gated.reshape(rows_all, cols_heads)
     partial_out = jnp.dot(gated_flat, w_out, preferred_element_type=jnp.float32)
     quarter = rows_all // mp_count
-    summed = lax.psum(partial_out, "mp")
+    summed = summed_here(partial_out, "mp")
     out_rows = lax.dynamic_slice_in_dim(summed, here_mp * quarter, quarter, 0)
     out_rows = out_rows + lax.dynamic_slice_in_dim(flat_rows, here_mp * quarter, quarter, 0).astype(
         jnp.float32

time: 695 us -> 757 us (1.089)
  blocking collectives: 0 us -> 107 us
  waiting for transfers between devices: 423 us -> 395 us
  starting transfers between devices: 48.5 us -> 29 us
    all_to_all x0 -> x3, blocking collectives: none -> 107 us  [the longest x1 77.8 us: per_device(): lax.all_to_all(looked, 'dp', split_axis=0, concat_axis=0, tiled=True)]
    psum x1 -> x0, waiting for transfers between devices: 34.2 us -> none  [per_device(): summed = lax.psum(partial_out, 'mp')]
    all_to_all x3 -> x0, waiting for transfers between devices: 32.3 us -> none  [the longest x1 27.9 us: per_device(): lax.all_to_all(looked, 'dp', split_axis=0, concat_axis=0, tiled=True)]
    all_to_all x3 -> x0, starting transfers between devices: 24 us -> none  [the longest x1 11.9 us: per_device(): lax.all_to_all(wanted, 'dp', split_axis=0, concat_axis=0, tiled=True)]
    all_to_all x1, waiting for transfers between devices: 3.51 us -> 26.2 us  [per_device(): lax.all_to_all(outgoing, 'dp', split_axis=0, concat_axis=0, tiled=True)]
    all_to_all x1, waiting for transfers between devices: 0.01 us -> 19.6 us  [per_device(): lax.all_to_all(lax.all_to_all(looked, 'dp', split_axis=0, concat_axis=0,...]
  transfers between devices with their start and end apart: 12 -> 9, of which waited for: 9 -> 7; matrix products, arithmetic and copies ran while one was open for 20% -> 18% of each run, Pallas kernels for 0% -> 0%
where the time goes in v1:
time: 757 us; the launch traced here: 746 us
  waiting for transfers between devices  395 us (52%)
  local copies, waits for them, and re-layouts  116 us (15%)
  blocking collectives  107 us (14%)
  other arithmetic  61.6 us (8%)
  starting transfers between devices  29 us (4%)
  matrix products  21.7 us (3%)
  between operations  15.7 us (2%)
    unnamed x6, waiting for transfers between devices  162 us
    reduce_scatter x1, waiting for transfers between devices, per_device(): lax.psum_scatter(w_out_part, 'dp', scatter_dimension=1, tiled=True)  112 us
    all_to_all x1, blocking collectives, per_device(): lax.all_to_all(looked, 'dp', split_axis=0, concat_axis=0, tiled=True)  77.8 us
    all_gather x1, waiting for transfers between devices, per_device(): lax.all_gather(out_grad.astype(jnp.bfloat16), 'mp', axis=0, tiled=True)  26.8 us
    all_to_all x1, waiting for transfers between devices, per_device(): lax.all_to_all(outgoing, 'dp', split_axis=0, concat_axis=0, tiled=True)  26.2 us
    all_to_all x1, waiting for transfers between devices, per_device(): lax.all_to_all(sending.reshape(dp_count, mp_count, capacity, width).astyp...  24.6 us
    all_gather x1, waiting for transfers between devices, per_device(): features = lax.all_gather(local_rows, 'mp', axis=2, tiled=True)  23.7 us
    all_to_all x1, blocking collectives, per_device(): lax.all_to_all(wanted, 'dp', split_axis=0, concat_axis=0, tiled=True)  20.5 us
  transfers between devices with their start and end apart: 9, of which 7 were waited for; matrix products, arithmetic and copies ran while one was open for 18% of the time, Pallas kernels for 0%

profile of v1, /device:TPU:8, one launch (start us, length us, event | category | flops | bytes accessed | tf_op | source)
XLA Modules:
  0.0 746.4 jit_solution(15027583963255597760)
XLA Ops:
  7.2 0.9 compare_select_fusion.7
  8.1 1.3 gather_fusion
  9.4 4.3 scatter_custom_fusion
  14.6 1.1 broadcast.800
  15.7 2.5 scatter_fusion
  18.2 11.9 %all-to-all-start = ((bf16[64,1,32,256]{3,2,1,0:T(8,128)(2,1)}), bf16[64,1,32,256]{3,2,1,0:T(8,128)(2,1)S(1)}, u32[]{:S(2)}, u32[]{:S(2)}) async-start(bf16[64,1,32,256]{3,2,1,0:T(8,128)(2,1)} %bitcast.7), calls=%async_computation | async-start | bytes 2097152 | tf_op jit(solution)/shard_map/all_to_all | solution.py:108
  30.3 1.4 gather_fusion.2
  32.0 26.2 %all-to-all-done = bf16[64,1,32,256]{3,2,1,0:T(8,128)(2,1)S(1)} async-done(((bf16[64,1,32,256]{3,2,1,0:T(8,128)(2,1)}), bf16[64,1,32,256]{3,2,1,0:T(8,128)(2,1)S(1)}, u32[]{:S(2)}, u32[]{:S(2)}) %all-to-all-start) | async-done | bytes 1048608 | tf_op jit(solution)/shard_map/all_to_all | solution.py:108
  58.8 0.8 broadcast_select_fusion.2
  60.9 23.7 %all-gather.5.cloned.1.call-done = bf16[16,32,1024]{2,1,0:T(8,128)(2,1)} async-done(((bf16[16,32,256]{2,1,0:T(8,128)(2,1)}), bf16[16,32,1024]{2,1,0:T(8,128)(2,1)}) %all-gather.5.cloned.1.call-update) | async-done | bytes 1048592 | tf_op jit(solution)/shard_map/all_gather | solution.py:121
  84.6 1.5 convert_reduce_fusion.1
  86.3 1.6 fusion.12
  88.0 2.8 fusion.16
  91.2 1.1 select_convert_fusion
  94.7 1.8 fusion.54
  98.2 4.3 scatter_custom_fusion.2
  102.6 5.9 gather_fusion.5
  109.3 20.5 %all_to_all.35 = s32[64,4,6]{2,1,0:T(4,128)S(1)} all-to-all(s32[64,4,6]{2,1,0:T(4,128)S(1)} %reshape.655), channel_id=1, replica_groups=mesh['dp'=64,'mp'=4] {'dp'}, dimensions={0} | all-to-all | bytes 12288 | tf_op jit(solution)/shard_map/all_to_all | solution.py:162
  130.0 9.1 %all_to_all.36 = s32[4,1,384]{2,1,0:T(1,128)S(1)} all-to-all(s32[4,1,384]{2,1,0:T(1,128)S(1)} %reshape.857), channel_id=1, replica_groups=mesh['dp'=64,'mp'=4] {'mp'}, dimensions={0} | all-to-all | bytes 12288 | tf_op jit(solution)/shard_map/all_to_all | solution.py:161
  140.8 5.9 gather_fusion.6
  146.7 6.3 gather.53
  153.1 2.6 broadcast_select_fusion
  155.7 6.2 copy.116
  162.0 77.8 %all_to_all.37 = bf16[64,4,6,1024]{3,1,2,0:T(4,128)(2,1)S(1)} all-to-all(bf16[64,4,6,1024]{3,1,2,0:T(4,128)(2,1)S(1)} %copy.116), channel_id=1, replica_groups=mesh['dp'=64,'mp'=4] {'dp'}, dimensions={0} | all-to-all | bytes 6291456 | tf_op jit(solution)/shard_map/all_to_all | solution.py:171
  239.7 3.4 copy.117
  243.2 5.4 all-to-all-start.4
  250.0 0.8 broadcast_in_dim.164
  251.8 0.9 broadcast_in_dim.175
  252.8 1.9 fusion.89
  254.7 9.9 %compare_convert_fusion = f32[128]{0:T(128)S(1)} fusion(s32[]{:T(128)} %bitcast.40, s32[]{:T(128)} %bitcast.41, s32[]{:T(128)} %bitcast.42, s32[]{:T(128)} %bitcast.43, s32[]{:T(128)} %bitcast.44, s32[]{:T(128)} %bitcast.46, s32[]{:T(128)} %bitcast.45, s32[]{:T(128)} %bitcast.23, s32[]{:T(128)} %bitcast.25, s32[]{:T(128)} %bitcast.27, s32[]{:T(128)} %bitcast.29, ...), kind=kLoop, calls=%fused_computation.196 | loop fusion | flops 8064 | bytes 580 | tf_op jit(solution)/shard_map/convert_element_type | solution.py:56
  266.0 19.6 %all-to-all-done.4 = bf16[64,4,6,1024]{3,0,2,1:T(8,128)(2,1)S(1)} async-done(((bf16[64,4,6,1024]{3,0,2,1:T(8,128)(2,1)}), bf16[64,4,6,1024]{3,0,2,1:T(8,128)(2,1)S(1)}, u32[]{:S(2)}, u32[]{:S(2)}) %all-to-all-start.4) | async-done | bytes 3145760 | tf_op jit(solution)/shard_map/all_to_all | solution.py:170
  285.7 3.8 copy.118
  289.4 4.9 reshape.657
  294.3 5.4 gather_fusion.7
  299.7 2.3 fusion.2
  302.2 5.9 reduce_sum.159
  308.1 1.4 multiply_reduce_fusion.2
  309.5 1.2 fusion.50
  310.8 1.8 fusion.10
  312.9 1.8 fusion.9
  314.8 1.7 fusion.7
  316.5 1.7 fusion.6
  318.2 5.8 gather_fusion.8
  324.0 6.2 gather.58
  330.2 4.6 fusion.1
  334.9 4.2 copy.133
  339.0 6.3 all-to-all-start.5
  345.6 0.9 divide_convert_fusion.1
  346.6 26.8 %all-gather.7.cloned.1.call-done = bf16[512,1024]{1,0:T(8,128)(2,1)} async-done(((bf16[128,1024]{1,0:T(8,128)(2,1)}), bf16[512,1024]{1,0:T(8,128)(2,1)}) %all-gather.7.cloned.1.call-update) | async-done | bytes 1048592 | tf_op jit(solution)/shard_map/all_gather | solution.py:201
  373.4 1.7 fusion.26
  378.8 1.9 copy.127
  380.8 2.9 reshape.662
  383.7 6.1 convolution_bitcast_fusion
  389.8 5.3 copy.129
  395.0 24.6 %all-to-all-done.5 = bf16[64,4,6,1024]{3,1,2,0:T(4,128)(2,1)} async-done(((bf16[64,4,6,1024]{3,1,2,0:T(4,128)(2,1)}), bf16[64,4,6,1024]{3,1,2,0:T(4,128)(2,1)}, u32[]{:S(2)}, u32[]{:S(2)}) %all-to-all-start.5) | async-done | bytes 3145760 | tf_op jit(solution)/shard_map/all_to_all | solution.py:184
  419.7 5.3 copy.134
  425.0 5.2 all-to-all-start.6
  430.2 2.8 fusion.52
  434.3 161.9 %all-reduce.7.cloned.1.call-done = f32[4,1024,256]{2,0,1:T(4,128)} async-done(((f32[4,1024,256]{2,0,1:T(4,128)}), f32[4,1024,256]{2,0,1:T(4,128)}) %all-reduce.7.cloned.1.call-update) | async-done | bytes 4194320
  596.2 0.8 constant_dynamic-slice_fusion
  597.7 5.1 copy.135
  602.8 8.4 %reshape.790 = f32[1536,1024]{1,0:T(8,128)} reshape(f32[64,4,6,1024]{3,2,1,0:T(8,128)} %copy.135) | data formatting | bytes 12582912 | tf_op jit(solution)/shard_map/reshape | solution.py:199
  611.3 16.1 %scatter_custom_fusion.3 = f32[512,1024]{1,0:T(8,128)} fusion(s32[1536]{0:T(1024)} %copy-done.37, f32[1536,1024]{1,0:T(8,128)} %reshape.790, f32[]{:T(128)} %constant.182.clone.1), kind=kCustom, calls=%fused_computation.68 | custom fusion | flops 1572864 | bytes 2097664 | tf_op jit(solution)/shard_map/scatter-add | solution.py:199
  627.3 112.4 %reduce-scatter.2.cloned.1.call-done = f32[256,16]{0,1:T(8,128)} async-done(((f32[256,1024]{0,1:T(8,128)}), f32[256,16]{0,1:T(8,128)}) %reduce-scatter.2.cloned.1.call-update) | async-done | bytes 16400 | tf_op jit(solution)/shard_map/reduce_scatter | solution.py:218
  (201 shorter events, 19.9 us)
Async XLA Ops:
  7.2 80.8 %copy-start = (bf16[4,1024,256]{2,1,0:T(8,128)(2,1)S(1)}, bf16[4,1024,256]{2,1,0:T(8,128)(2,1)}, u32[]{:S(2)}) copy-start(bf16[4,1024,256]{2,1,0:T(8,128)(2,1)} %param.14) | copy-start | bytes 6291460
  7.2 8.5 %copy-start.22 = (bf16[16,32,256]{2,1,0:T(8,128)(2,1)S(1)}, bf16[16,32,256]{2,1,0:T(8,128)(2,1)}, u32[]{:S(2)}) copy-start(bf16[16,32,256]{2,1,0:T(8,128)(2,1)} %param.8) | copy-start | bytes 786436
  18.2 40.1 %all-to-all-start = ((bf16[64,1,32,256]{3,2,1,0:T(8,128)(2,1)}), bf16[64,1,32,256]{3,2,1,0:T(8,128)(2,1)S(1)}, u32[]{:S(2)}, u32[]{:S(2)}) async-start(bf16[64,1,32,256]{3,2,1,0:T(8,128)(2,1)} %bitcast.7), calls=%async_computation | async-start | bytes 2097152 | tf_op jit(solution)/shard_map/all_to_all | solution.py:108
  30.1 54.5 %all-gather.5.cloned.1.call-start = ((), (), s32[]{:S(2)}) async-start(), calls=%async_computation.8 | async-start | bytes 1310720 | tf_op jit(solution)/shard_map/all_gather | solution.py:121
  30.3 29.4 %copy-start.3 = (s32[1024]{0:T(1024)S(1)}, s32[1024]{0:T(1024)}, u32[]{:S(2)}) copy-start(s32[1024]{0:T(1024)} %param.9) | copy-start | bytes 12292
  59.7 242.5 %all-gather.9.cloned.1.call-start = ((), (), s32[]{:S(2)}) async-start(), calls=%async_computation.11 | async-start | bytes 10485760 | tf_op jit(solution)/shard_map/all_gather | solution.py:13
  60.4 0.5 copy-start.23
  60.4 30.8 %copy-start.47 = (f32[16]{0:T(128)}, f32[16]{0:T(128)S(1)}, u32[]{:S(2)}) copy-start(f32[16]{0:T(128)S(1)} %convert_element_type.130) | copy-start | bytes 196
  60.9 30.2 %copy-start.33 = (pred[16,32,32]{2,1,0:T(8,128)(4,1)}, pred[16,32,32]{2,1,0:T(8,128)(4,1)S(1)}, u32[]{:S(2)}) copy-start(pred[16,32,32]{2,1,0:T(8,128)(4,1)S(1)} %broadcast_and_fusion) | copy-start | bytes 49156
  84.6 3.4 copy-start.10
  86.3 4.5 copy-start.42
  88.0 2.8 copy-start.44
  91.0 1.3 copy-start.14
  91.1 1.3 copy-start.16
  91.2 1.2 copy-start.18
  92.3 1.5 copy-start.20
  92.3 2.4 copy-start.12
  92.7 3.8 copy-start.6
  93.2 0.7 copy-start.26
  93.8 2.7 copy-start.24
  94.1 2.4 copy-start.8
  94.7 1.8 copy-start.40
  94.7 2.0 copy-start.41
  96.9 5.6 copy-start.38
  97.6 5.0 copy-start.36
  97.6 0.6 copy-start.39
  102.5 5.9 copy-start.28
  102.6 5.9 copy-start.29
  102.6 38.2 %copy-start.2 = (bf16[512,1024]{1,0:T(8,128)(2,1)S(1)}, bf16[512,1024]{1,0:T(8,128)(2,1)}, u32[]{:S(2)}) copy-start(bf16[512,1024]{1,0:T(8,128)(2,1)} %param.13) | copy-start | bytes 3145732
  140.8 5.9 copy-start.37
  243.2 42.5 %all-to-all-start.4 = ((bf16[64,4,6,1024]{3,0,2,1:T(8,128)(2,1)}), bf16[64,4,6,1024]{3,0,2,1:T(8,128)(2,1)S(1)}, u32[]{:S(2)}, u32[]{:S(2)}) async-start(bf16[64,4,6,1024]{3,0,2,1:T(8,128)(2,1)} %copy.117), calls=%async_computation.4 | async-start | bytes 6291456 | tf_op jit(solution)/shard_map/all_to_all | solution.py:170
  302.1 8.6 %copy-start.35 = (f32[128,8]{1,0:T(8,128)}, f32[128,8]{1,0:T(8,128)S(1)}, u32[]{:S(2)}) copy-start(f32[128,8]{1,0:T(8,128)S(1)} %sqrt.53) | copy-start | bytes 12292
  302.2 8.6 %copy-start.32 = (pred[128,8]{1,0:T(8,128)(4,1)S(1)}, pred[128,8]{1,0:T(8,128)(4,1)}, u32[]{:S(2)}) copy-start(pred[128,8]{1,0:T(8,128)(4,1)} %compare_and_fusion) | copy-start | bytes 3076
  308.1 2.7 copy-start.4
  314.8 1.7 copy-start.5
  316.5 1.7 copy-start.30
  339.0 80.6 %all-to-all-start.5 = ((bf16[64,4,6,1024]{3,1,2,0:T(4,128)(2,1)}), bf16[64,4,6,1024]{3,1,2,0:T(4,128)(2,1)}, u32[]{:S(2)}, u32[]{:S(2)}) async-start(bf16[64,4,6,1024]{3,1,2,0:T(4,128)(2,1)} %copy.133), calls=%async_computation.6 | async-start | bytes 6291456 | tf_op jit(solution)/shard_map/all_to_all | solution.py:184
  345.4 28.0 %copy-start.13 = (bf16[256,1024]{1,0:T(8,128)(2,1)S(1)}, bf16[256,1024]{1,0:T(8,128)(2,1)}, u32[]{:S(2)}) copy-start(bf16[256,1024]{1,0:T(8,128)(2,1)} %param.15) | copy-start | bytes 1572868
  345.4 28.0 %all-gather.7.cloned.1.call-start = ((), (), s32[]{:S(2)}) async-start(), calls=%async_computation.9 | async-start | bytes 1310720 | tf_op jit(solution)/shard_map/all_gather | solution.py:201
  345.6 29.8 %copy-start.7 = (f32[16,32,2,128]{3,1,2,0:T(8,128)S(1)}, f32[16,32,2,128]{3,1,2,0:T(8,128)}, u32[]{:S(2)}) copy-start(f32[16,32,2,128]{3,1,2,0:T(8,128)} %copy-done.6) | copy-start | bytes 1572868
  345.6 29.8 %copy-start.9 = (f32[16,32,2,128]{3,2,1,0:T(2,128)S(1)}, f32[16,32,2,128]{3,2,1,0:T(2,128)}, u32[]{:S(2)}) copy-start(f32[16,32,2,128]{3,2,1,0:T(2,128)} %copy-done.8) | copy-start | bytes 1572868
  345.6 29.8 %copy-start.31 = (f32[16,32,2]{1,2,0:T(2,128)S(1)}, f32[16,32,2]{1,2,0:T(2,128)}, u32[]{:S(2)}) copy-start(f32[16,32,2]{1,2,0:T(2,128)} %get-tuple-element.29) | copy-start | bytes 12292
  346.5 29.4 %copy-start.27 = (f32[16,32,2]{1,2,0:T(2,128)S(1)}, f32[16,32,2]{1,2,0:T(2,128)}, u32[]{:S(2)}) copy-start(f32[16,32,2]{1,2,0:T(2,128)} %copy-done.26) | copy-start | bytes 12292
  346.5 29.5 %copy-start.25 = (f32[16,32,2]{1,2,0:T(2,128)S(1)}, f32[16,32,2]{1,2,0:T(2,128)}, u32[]{:S(2)}) copy-start(f32[16,32,2]{1,2,0:T(2,128)} %copy-done.24) | copy-start | bytes 12292
  346.6 249.7 %all-reduce.7.cloned.1.call-start = ((), (), s32[]{:S(2)}) async-start(), calls=%async_computation.12 | async-start | bytes 8388608
  375.4 1.3 copy-start.19
  375.4 1.3 copy-start.34
  375.4 1.3 copy-start.48
  375.4 1.3 copy-start.49
  376.7 1.0 copy-start.17
  376.7 1.2 copy-start.15
  376.7 1.4 copy-start.21
  380.7 2.9 copy-start.11
  380.7 2.9 copy-start.43
  380.8 2.9 copy-start.45
  425.0 172.7 %all-to-all-start.6 = ((bf16[64,4,6,1024]{3,0,2,1:T(8,128)(2,1)}), bf16[64,4,6,1024]{3,0,2,1:T(8,128)(2,1)S(1)}, u32[]{:S(2)}, u32[]{:S(2)}) async-start(bf16[64,4,6,1024]{3,0,2,1:T(8,128)(2,1)} %copy.134), calls=%async_computation.7 | async-start | bytes 6291456 | tf_op jit(solution)/shard_map/all_to_all | solution.py:183
  430.2 2.8 copy-start.46
  430.2 309.5 %reduce-scatter.2.cloned.1.call-start = ((), (), s32[]{:S(2)}) async-start(), calls=%async_computation.10 | async-start | bytes 1064960 | tf_op jit(solution)/shard_map/reduce_scatter | solution.py:218
  602.8 136.9 %copy-start.1 = (bf16[4,1024,256]{2,1,0:T(8,128)(2,1)S(1)}, bf16[4,1024,256]{2,1,0:T(8,128)(2,1)}, u32[]{:S(2)}) copy-start(bf16[4,1024,256]{2,1,0:T(8,128)(2,1)} %param.14) | copy-start | bytes 6291460
Sparse Core Ops, SparseCore 0:
  59.8 24.8 all-gather.4
  96.7 87.2 all-gather.8
  348.0 25.3 all-gather.6
  395.2 201.0 all-reduce.6
  600.6 139.0 reduce-scatter.1
